TPU v7x, 512 devices: a whole 4x4x16 slice. The times are simulated.
512 devices in a mesh: sub: 16 (over z), leaf: 32 (over y, x, core).
Axes of the slice: x: 4, y: 4, z: 16, core: 2. Of those that a mesh axis runs over, the one named last changes fastest.
Arguments:
- shift: float32 [1], replicated, may hold values from 0.5 to 2
- self_terms: float32 [524288], P(('leaf', 'sub')), may hold values from 1 to 2
- order: int32 [512, 1024], P(('leaf', 'sub')), may hold values from 0 to 1023, each once within a row
- split: int32 [512], P(('leaf', 'sub')), may hold values from 256 to 768
- coupling: bfloat16 [524288, 768], P(('leaf', 'sub')), as said below
- higher: bfloat16 [524288, 512], P(('leaf', 'sub'))
Outputs:
- applied_higher: bfloat16 [524288, 512], P(('leaf', 'sub'))
Inputs may be any that keep to these rules, and one draw needn't show every extreme that they name: `coupling`: at every node of every level, the symmetric matrix made of diag and the blocks U V^T and V U^T of this and lower levels is positive definite.
All inputs are finite; a program needn't handle non-finite values.
Results may differ from a plain program's by a relative error of at most 0.001.
The roundings to bfloat16 on the way count: a program that leaves them out, or rounds other values in their place, can miss the bound.
Values sent between devices are 32-bit elements; how exact they have to be, the bound alone decides.
A program may use at most 64 MiB of HBM per device.

v0:
```python
import jax
import jax.numpy as jnp
from jax import lax
from jax.sharding import PartitionSpec as P

RANK = 128


def from_partner(value, axis, stride):
    mask = 2**stride
    pairs = [(source, source ^ mask) for source in range(lax.axis_size(axis))]
    return lax.ppermute(value, axis, pairs)


def factor_solve(factor, target):
    lower_part = lax.linalg.triangular_solve(factor, target, left_side=True, lower=True)
    return lax.linalg.triangular_solve(
        factor, lower_part, left_side=True, lower=True, transpose_a=True
    )


def core_terms(left_sum, right_sum):
    width = left_sum.shape[0]
    first = left_sum[:, :width]
    projected = left_sum[:, width:]
    second = right_sum[:, :width]
    beyond = right_sum[:, width:]
    identity_block = jnp.eye(width, dtype=jnp.float32)
    first_factor = jnp.linalg.cholesky(first)
    first_inverse = factor_solve(first_factor, identity_block)
    schur_factor = jnp.linalg.cholesky(first_inverse - second)
    target = beyond - jnp.dot(second, projected, precision=lax.Precision.HIGHEST)
    back = factor_solve(schur_factor, target) - projected
    across = beyond + jnp.dot(second, back, precision=lax.Precision.HIGHEST)
    return (across, back)


def project_rows(basis, columns):
    return lax.dot_general(
        basis, columns, (((0,), (0,)), ((), ())), preferred_element_type=jnp.float32
    )


def node_step(columns, mine, other, is_left):
    left_sum = jnp.where(is_left, mine, other)
    right_sum = jnp.where(is_left, other, mine)
    across, back = core_terms(left_sum, right_sum)
    coefficient = jnp.where(is_left, -across, back).astype(jnp.bfloat16)
    update = columns[:, RANK:].astype(jnp.float32) + jnp.dot(
        columns[:, :RANK], coefficient, preferred_element_type=jnp.float32
    )
    return update.astype(jnp.bfloat16)


def per_device(shift, self_terms, order, split, coupling, higher):
    sub_bits = lax.axis_size("sub").bit_length() - 1
    diagonal = shift[0] + self_terms
    joined = jnp.concatenate([coupling, higher], axis=1).astype(jnp.float32)
    columns = (joined / diagonal[:, None]).astype(jnp.bfloat16)
    inside = (order[0] < split[0]).astype(jnp.bfloat16)[:, None]
    outside = 1 - inside
    basis = coupling[:, :RANK]
    left_sum = project_rows(basis * inside, columns)
    right_sum = project_rows(basis * outside, columns)
    across, back = core_terms(left_sum, right_sum)
    own = columns[:, :RANK]
    update = columns[:, RANK:].astype(jnp.float32)
    update = update + jnp.dot(
        own * inside, (-across).astype(jnp.bfloat16), preferred_element_type=jnp.float32
    )
    update = update + jnp.dot(
        own * outside, back.astype(jnp.bfloat16), preferred_element_type=jnp.float32
    )
    columns = update.astype(jnp.bfloat16)
    position = lax.axis_index("sub")
    for level in range(1, sub_bits + 1):
        basis = coupling[:, level * RANK : (level + 1) * RANK]
        partial_value = project_rows(basis, columns)
        stride = 2 ** (level - 1)
        mine = partial_value
        for bit in range(level - 1):
            mine = mine + from_partner(mine, "sub", bit)
        other = from_partner(mine, "sub", level - 1)
        is_left = position // stride % 2 == 0
        columns = node_step(columns, mine, other, is_left)
    top = sub_bits + 1
    basis = coupling[:, top * RANK : (top + 1) * RANK]
    partial_value = project_rows(basis, columns)
    mine = lax.psum(partial_value, "sub")
    other = from_partner(mine, "leaf", 0)
    is_left = lax.axis_index("leaf") % 2 == 0
    return node_step(columns, mine, other, is_left)


def solution(mesh):
    in_specs = (
        P(),
        P(("leaf", "sub")),
        P(("leaf", "sub"), None),
        P(("leaf", "sub")),
        P(("leaf", "sub"), None),
        P(("leaf", "sub"), None),
    )
    out_specs = P(("leaf", "sub"), None)
    return jax.shard_map(
        per_device, mesh=mesh, in_specs=in_specs, out_specs=out_specs, check_vma=False
    )
```

profile of v0, /device:TPU:1, one launch (start us, length us, event | category | flops | bytes accessed | tf_op | source)
XLA Modules:
  0.0 782.3 jit_solution(3534729396626597273)
XLA Ops:
  9.2 2.3 divide_convert_fusion
  11.6 1.6 fusion.35
  13.2 1.6 fusion.37
  17.2 11.7 %cholesky.194 = f32[128,128]{1,0:T(8,128)S(1)} custom-call(f32[128,128]{1,0:T(8,128)S(1)} %fusion.114), custom_call_target="Cholesky" | custom-call | tf_op jit(solution)/shard_map/jit(cholesky)/cholesky | solution.py:29
  30.1 9.8 %custom-call.55 = f32[1,128,128]{1,2,0:T(8,128)S(1)} custom-call(f32[1,128,128]{2,1,0:T(8,128)S(1)} %fusion.61), custom_call_target="InvertDiagBlocksLowerTriangular" | custom-call | tf_op jit(solution)/shard_map/triangular_solve/custom-call.2 | solution.py:17
  42.2 11.7 %cholesky.205 = f32[128,128]{1,0:T(8,128)S(1)} custom-call(f32[128,128]{1,0:T(8,128)S(1)} %fusion.111), custom_call_target="Cholesky" | custom-call | tf_op jit(solution)/shard_map/jit(cholesky)/cholesky | solution.py:31
  55.4 9.8 %custom-call.38 = f32[1,128,128]{1,2,0:T(8,128)S(1)} custom-call(f32[1,128,128]{2,1,0:T(8,128)S(1)} %fusion.62), custom_call_target="InvertDiagBlocksLowerTriangular" | custom-call | tf_op jit(solution)/shard_map/triangular_solve | solution.py:17
  65.2 1.7 fusion.109
  67.6 1.7 fusion.2
  71.0 2.0 convolution_bitcast_fusion
  73.0 4.4 collective-permute-start
  77.4 8.5 %collective-permute-done = f32[128,1152]{0,1:T(8,128)S(1)} collective-permute-done((f32[128,1152]{0,1:T(8,128)S(1)}, f32[128,1152]{0,1:T(8,128)S(1)}, u32[]{:S(2)}, u32[]{:S(2)}) %collective-permute-start) | collective-permute-done | bytes 589856 | tf_op jit(solution)/shard_map/ppermute | solution.py:12
  86.1 11.7 %cholesky.216 = f32[128,128]{1,0:T(8,128)S(1)} custom-call(f32[128,128]{1,0:T(8,128)S(1)} %fusion.107), custom_call_target="Cholesky" | custom-call | tf_op jit(solution)/shard_map/jit(cholesky)/cholesky | solution.py:29
  99.2 9.8 %custom-call.57 = f32[1,128,128]{1,2,0:T(8,128)S(1)} custom-call(f32[1,128,128]{2,1,0:T(8,128)S(1)} %fusion.63), custom_call_target="InvertDiagBlocksLowerTriangular" | custom-call | tf_op jit(solution)/shard_map/triangular_solve/custom-call.2 | solution.py:17
  110.3 11.7 %cholesky.227 = f32[128,128]{1,0:T(8,128)S(1)} custom-call(f32[128,128]{1,0:T(8,128)S(1)} %fusion.104), custom_call_target="Cholesky" | custom-call | tf_op jit(solution)/shard_map/jit(cholesky)/cholesky | solution.py:31
  123.3 21.7 %custom-call.39 = f32[1,128,128]{1,2,0:T(8,128)S(1)} custom-call(f32[1,128,128]{2,1,0:T(8,128)S(1)} %fusion.64), custom_call_target="InvertDiagBlocksLowerTriangular" | custom-call | tf_op jit(solution)/shard_map/triangular_solve | solution.py:17
  147.3 2.4 add_convert_fusion
  151.0 4.1 collective-permute-start.1
  155.1 7.0 collective-permute-done.1
  162.2 12.1 %collective-permute-start.2 = (f32[128,1024]{0,1:T(8,128)S(1)}, f32[128,1024]{0,1:T(8,128)}, u32[]{:S(2)}, u32[]{:S(2)}) collective-permute-start(f32[128,1024]{0,1:T(8,128)S(1)} %add.127), channel_id=1, source_target_pairs={{0,64},{32,96},{64,0},{96,32},{128,192},{160,224},{192,128},{224,1... | collective-permute-start | bytes 1572872 | tf_op jit(solution)/shard_map/ppermute | solution.py:12
  174.4 22.8 %collective-permute-done.2 = f32[128,1024]{0,1:T(8,128)} collective-permute-done((f32[128,1024]{0,1:T(8,128)S(1)}, f32[128,1024]{0,1:T(8,128)}, u32[]{:S(2)}, u32[]{:S(2)}) %collective-permute-start.2) | collective-permute-done | bytes 524320 | tf_op jit(solution)/shard_map/ppermute | solution.py:12
  198.5 11.7 %cholesky.238 = f32[128,128]{1,0:T(8,128)S(1)} custom-call(f32[128,128]{1,0:T(8,128)S(1)} %fusion.100), custom_call_target="Cholesky" | custom-call | tf_op jit(solution)/shard_map/jit(cholesky)/cholesky | solution.py:29
  211.6 9.8 %custom-call.59 = f32[1,128,128]{1,2,0:T(8,128)S(1)} custom-call(f32[1,128,128]{2,1,0:T(8,128)S(1)} %fusion.65), custom_call_target="InvertDiagBlocksLowerTriangular" | custom-call | tf_op jit(solution)/shard_map/triangular_solve/custom-call.2 | solution.py:17
  222.6 11.7 %cholesky.249 = f32[128,128]{1,0:T(8,128)S(1)} custom-call(f32[128,128]{1,0:T(8,128)S(1)} %fusion.97), custom_call_target="Cholesky" | custom-call | tf_op jit(solution)/shard_map/jit(cholesky)/cholesky | solution.py:31
  235.7 10.2 %custom-call.40 = f32[1,128,128]{1,2,0:T(8,128)S(1)} custom-call(f32[1,128,128]{2,1,0:T(8,128)S(1)} %fusion.66), custom_call_target="InvertDiagBlocksLowerTriangular" | custom-call | tf_op jit(solution)/shard_map/triangular_solve | solution.py:17
  247.9 2.2 add_convert_fusion.1
  250.9 2.9 collective-permute-start.3
  253.8 9.7 %collective-permute-done.3 = f32[128,896]{0,1:T(8,128)S(1)} collective-permute-done((f32[128,896]{0,1:T(8,128)S(1)}, f32[128,896]{0,1:T(8,128)S(1)}, u32[]{:S(2)}, u32[]{:S(2)}) %collective-permute-start.3) | collective-permute-done | bytes 458784 | tf_op jit(solution)/shard_map/ppermute | solution.py:12
  263.6 5.7 collective-permute-start.4
  269.3 19.9 %collective-permute-done.4 = f32[128,896]{0,1:T(8,128)S(1)} collective-permute-done((f32[128,896]{0,1:T(8,128)S(1)}, f32[128,896]{0,1:T(8,128)S(1)}, u32[]{:S(2)}, u32[]{:S(2)}) %collective-permute-start.4) | collective-permute-done | bytes 458784 | tf_op jit(solution)/shard_map/ppermute | solution.py:12
  289.3 8.8 %collective-permute-start.5 = (f32[128,896]{0,1:T(8,128)S(1)}, f32[128,896]{0,1:T(8,128)S(1)}, u32[]{:S(2)}, u32[]{:S(2)}) collective-permute-start(f32[128,896]{0,1:T(8,128)S(1)} %add.132), channel_id=1, source_target_pairs={{0,128},{32,160},{64,192},{96,224},{128,0},{160,32},{192,64},{224,... | collective-permute-start | bytes 1376264 | tf_op jit(solution)/shard_map/ppermute | solution.py:12
  298.1 39.4 %collective-permute-done.5 = f32[128,896]{0,1:T(8,128)S(1)} collective-permute-done((f32[128,896]{0,1:T(8,128)S(1)}, f32[128,896]{0,1:T(8,128)S(1)}, u32[]{:S(2)}, u32[]{:S(2)}) %collective-permute-start.5) | collective-permute-done | bytes 458784 | tf_op jit(solution)/shard_map/ppermute | solution.py:12
  337.7 11.7 %cholesky.260 = f32[128,128]{1,0:T(8,128)S(1)} custom-call(f32[128,128]{1,0:T(8,128)S(1)} %fusion.93), custom_call_target="Cholesky" | custom-call | tf_op jit(solution)/shard_map/jit(cholesky)/cholesky | solution.py:29
  350.7 9.8 %custom-call.61 = f32[1,128,128]{1,2,0:T(8,128)S(1)} custom-call(f32[1,128,128]{2,1,0:T(8,128)S(1)} %fusion.67), custom_call_target="InvertDiagBlocksLowerTriangular" | custom-call | tf_op jit(solution)/shard_map/triangular_solve/custom-call.2 | solution.py:17
  361.7 11.7 %cholesky.271 = f32[128,128]{1,0:T(8,128)S(1)} custom-call(f32[128,128]{1,0:T(8,128)S(1)} %fusion.90), custom_call_target="Cholesky" | custom-call | tf_op jit(solution)/shard_map/jit(cholesky)/cholesky | solution.py:31
  374.8 9.9 %custom-call.41 = f32[1,128,128]{1,2,0:T(8,128)S(1)} custom-call(f32[1,128,128]{2,1,0:T(8,128)S(1)} %fusion.68), custom_call_target="InvertDiagBlocksLowerTriangular" | custom-call | tf_op jit(solution)/shard_map/triangular_solve | solution.py:17
  386.6 2.1 add_convert_fusion.2
  389.2 1.9 collective-permute-start.6
  391.2 10.1 %collective-permute-done.6 = f32[128,768]{0,1:T(8,128)S(1)} collective-permute-done((f32[128,768]{0,1:T(8,128)S(1)}, f32[128,768]{0,1:T(8,128)S(1)}, u32[]{:S(2)}, u32[]{:S(2)}) %collective-permute-start.6) | collective-permute-done | bytes 393248 | tf_op jit(solution)/shard_map/ppermute | solution.py:12
  401.4 1.9 collective-permute-start.7
  403.3 20.3 %collective-permute-done.7 = f32[128,768]{0,1:T(8,128)S(1)} collective-permute-done((f32[128,768]{0,1:T(8,128)S(1)}, f32[128,768]{0,1:T(8,128)S(1)}, u32[]{:S(2)}, u32[]{:S(2)}) %collective-permute-start.7) | collective-permute-done | bytes 393248 | tf_op jit(solution)/shard_map/ppermute | solution.py:12
  423.7 4.3 collective-permute-start.8
  428.0 35.9 %collective-permute-done.8 = f32[128,768]{0,1:T(8,128)S(1)} collective-permute-done((f32[128,768]{0,1:T(8,128)S(1)}, f32[128,768]{0,1:T(8,128)S(1)}, u32[]{:S(2)}, u32[]{:S(2)}) %collective-permute-start.8) | collective-permute-done | bytes 393248 | tf_op jit(solution)/shard_map/ppermute | solution.py:12
  464.7 19.0 %collective-permute-start.9 = (f32[128,768]{0,1:T(8,128)}, f32[128,768]{0,1:T(8,128)}, u32[]{:S(2)}, u32[]{:S(2)}) collective-permute-start(f32[128,768]{0,1:T(8,128)} %add.138), channel_id=1, source_target_pairs={{0,256},{32,288},{64,320},{96,352},{128,384},{160,416},{192,448},{... | collective-permute-start | bytes 1179656 | tf_op jit(solution)/shard_map/ppermute | solution.py:12
  483.7 14.6 %collective-permute-done.9 = f32[128,768]{0,1:T(8,128)} collective-permute-done((f32[128,768]{0,1:T(8,128)}, f32[128,768]{0,1:T(8,128)}, u32[]{:S(2)}, u32[]{:S(2)}) %collective-permute-start.9) | collective-permute-done | bytes 393248 | tf_op jit(solution)/shard_map/ppermute | solution.py:12
  498.3 1.9 broadcast_select_fusion.7
  500.9 1.6 copy.24
  503.9 13.2 %cholesky.282 = f32[128,128]{1,0:T(8,128)} custom-call(f32[128,128]{1,0:T(8,128)} %fusion.86), custom_call_target="Cholesky" | custom-call | tf_op jit(solution)/shard_map/jit(cholesky)/cholesky | solution.py:29
  518.6 2.1 fusion.69
  520.7 11.3 %custom-call.63 = f32[1,128,128]{1,2,0:T(8,128)} custom-call(f32[1,128,128]{2,1,0:T(8,128)} %fusion.69), custom_call_target="InvertDiagBlocksLowerTriangular" | custom-call | tf_op jit(solution)/shard_map/triangular_solve/custom-call.2 | solution.py:17
  533.1 2.1 convolution_subtract_fusion.9
  535.2 1.8 convolution_subtract_fusion.13
  537.0 1.6 copy.26
  540.1 13.2 %cholesky.293 = f32[128,128]{1,0:T(8,128)} custom-call(f32[128,128]{1,0:T(8,128)} %fusion.83), custom_call_target="Cholesky" | custom-call | tf_op jit(solution)/shard_map/jit(cholesky)/cholesky | solution.py:31
  554.8 2.1 fusion.70
  556.9 11.4 %custom-call.42 = f32[1,128,128]{1,2,0:T(8,128)} custom-call(f32[1,128,128]{2,1,0:T(8,128)} %fusion.70), custom_call_target="InvertDiagBlocksLowerTriangular" | custom-call | tf_op jit(solution)/shard_map/triangular_solve | solution.py:17
  569.9 1.5 convolution_subtract_fusion.8
  575.8 133.2 %all-reduce.2.cloned.1.call-done = f32[128,640]{0,1:T(8,128)} async-done(((f32[128,640]{0,1:T(8,128)}), f32[128,640]{0,1:T(8,128)}) %all-reduce.2.cloned.1.call-update) | async-done | bytes 327696 | tf_op jit(solution)/shard_map/psum | solution.py:89
  708.9 12.3 %collective-permute-start.10 = (f32[128,640]{0,1:T(8,128)}, f32[128,640]{0,1:T(8,128)S(1)}, u32[]{:S(2)}, u32[]{:S(2)}) collective-permute-start(f32[128,640]{0,1:T(8,128)} %all-reduce.2.cloned.1.call-done), channel_id=1, source_target_pairs={{0,1},{1,0},{2,3},{3,2},{4,5},{5,4},{6,7},{7,6},{8,9},{9,8},{10,11... | collective-permute-start | bytes 983048 | tf_op jit(solution)/shard_map/ppermute | solution.py:12
  723.9 11.7 %cholesky.304 = f32[128,128]{1,0:T(8,128)S(1)} custom-call(f32[128,128]{1,0:T(8,128)S(1)} %fusion.79), custom_call_target="Cholesky" | custom-call | tf_op jit(solution)/shard_map/jit(cholesky)/cholesky | solution.py:29
  736.9 9.8 %custom-call.65 = f32[1,128,128]{1,2,0:T(8,128)S(1)} custom-call(f32[1,128,128]{2,1,0:T(8,128)S(1)} %fusion.71), custom_call_target="InvertDiagBlocksLowerTriangular" | custom-call | tf_op jit(solution)/shard_map/triangular_solve/custom-call.2 | solution.py:17
  747.8 11.7 %cholesky.315 = f32[128,128]{1,0:T(8,128)S(1)} custom-call(f32[128,128]{1,0:T(8,128)S(1)} %fusion.76), custom_call_target="Cholesky" | custom-call | tf_op jit(solution)/shard_map/jit(cholesky)/cholesky | solution.py:31
  760.9 10.0 %custom-call.43 = f32[1,128,128]{1,2,0:T(8,128)S(1)} custom-call(f32[1,128,128]{2,1,0:T(8,128)S(1)} %fusion.72), custom_call_target="InvertDiagBlocksLowerTriangular" | custom-call | tf_op jit(solution)/shard_map/triangular_solve | solution.py:17
  772.3 2.7 add_convert_fusion.4
  (130 shorter events, 55.2 us)
Async XLA Ops:
  6.5 702.4 %all-reduce.2.cloned.1.call-start = ((), (), s32[]{:S(2)}) async-start(), calls=%async_computation | async-start | bytes 655360 | tf_op jit(solution)/shard_map/psum | solution.py:89
  14.8 0.8 copy-start.5
  71.0 2.0 copy-start
  73.0 12.9 %collective-permute-start = (f32[128,1152]{0,1:T(8,128)S(1)}, f32[128,1152]{0,1:T(8,128)S(1)}, u32[]{:S(2)}, u32[]{:S(2)}) collective-permute-start(f32[128,1152]{0,1:T(8,128)S(1)} %convolution_bitcast_fusion), channel_id=1, source_target_pairs={{0,32},{32,0},{64,96},{96,64},{128,160},{160,128},{192,224},{224,1... | collective-permute-start | bytes 1769480 | tf_op jit(solution)/shard_map/ppermute | solution.py:12
  146.7 3.0 copy-start.1
  149.7 1.4 copy-start.2
  151.0 11.1 %collective-permute-start.1 = (f32[128,1024]{0,1:T(8,128)S(1)}, f32[128,1024]{0,1:T(8,128)S(1)}, u32[]{:S(2)}, u32[]{:S(2)}) collective-permute-start(f32[128,1024]{0,1:T(8,128)S(1)} %convolution_bitcast_fusion.1), channel_id=1, source_target_pairs={{0,32},{32,0},{64,96},{96,64},{128,160},{160,128},{192,224},{224,1... | collective-permute-start | bytes 1572872 | tf_op jit(solution)/shard_map/ppermute | solution.py:12
  162.2 35.0 %collective-permute-start.2 = (f32[128,1024]{0,1:T(8,128)S(1)}, f32[128,1024]{0,1:T(8,128)}, u32[]{:S(2)}, u32[]{:S(2)}) collective-permute-start(f32[128,1024]{0,1:T(8,128)S(1)} %add.127), channel_id=1, source_target_pairs={{0,64},{32,96},{64,0},{96,32},{128,192},{160,224},{192,128},{224,1... | collective-permute-start | bytes 1572872 | tf_op jit(solution)/shard_map/ppermute | solution.py:12
  250.2 39.1 %copy-start.3 = (bf16[1024,896]{1,0:T(8,128)(2,1)}, bf16[1024,896]{1,0:T(8,128)(2,1)S(1)}, u32[]{:S(2)}) copy-start(bf16[1024,896]{1,0:T(8,128)(2,1)S(1)} %add_convert_fusion.1) | copy-start | bytes 5505028
  250.9 12.7 %collective-permute-start.3 = (f32[128,896]{0,1:T(8,128)S(1)}, f32[128,896]{0,1:T(8,128)S(1)}, u32[]{:S(2)}, u32[]{:S(2)}) collective-permute-start(f32[128,896]{0,1:T(8,128)S(1)} %convolution_bitcast_fusion.2), channel_id=1, source_target_pairs={{0,32},{32,0},{64,96},{96,64},{128,160},{160,128},{192,224},{224,1... | collective-permute-start | bytes 1376264 | tf_op jit(solution)/shard_map/ppermute | solution.py:12
  263.6 25.6 %collective-permute-start.4 = (f32[128,896]{0,1:T(8,128)S(1)}, f32[128,896]{0,1:T(8,128)S(1)}, u32[]{:S(2)}, u32[]{:S(2)}) collective-permute-start(f32[128,896]{0,1:T(8,128)S(1)} %add.131), channel_id=1, source_target_pairs={{0,64},{32,96},{64,0},{96,32},{128,192},{160,224},{192,128},{224,1... | collective-permute-start | bytes 1376264 | tf_op jit(solution)/shard_map/ppermute | solution.py:12
  289.3 48.2 %collective-permute-start.5 = (f32[128,896]{0,1:T(8,128)S(1)}, f32[128,896]{0,1:T(8,128)S(1)}, u32[]{:S(2)}, u32[]{:S(2)}) collective-permute-start(f32[128,896]{0,1:T(8,128)S(1)} %add.132), channel_id=1, source_target_pairs={{0,128},{32,160},{64,192},{96,224},{128,0},{160,32},{192,64},{224,... | collective-permute-start | bytes 1376264 | tf_op jit(solution)/shard_map/ppermute | solution.py:12
  389.2 12.1 %collective-permute-start.6 = (f32[128,768]{0,1:T(8,128)S(1)}, f32[128,768]{0,1:T(8,128)S(1)}, u32[]{:S(2)}, u32[]{:S(2)}) collective-permute-start(f32[128,768]{0,1:T(8,128)S(1)} %convolution_bitcast_fusion.3), channel_id=1, source_target_pairs={{0,32},{32,0},{64,96},{96,64},{128,160},{160,128},{192,224},{224,1... | collective-permute-start | bytes 1179656 | tf_op jit(solution)/shard_map/ppermute | solution.py:12
  401.4 22.2 %collective-permute-start.7 = (f32[128,768]{0,1:T(8,128)S(1)}, f32[128,768]{0,1:T(8,128)S(1)}, u32[]{:S(2)}, u32[]{:S(2)}) collective-permute-start(f32[128,768]{0,1:T(8,128)S(1)} %add.136), channel_id=1, source_target_pairs={{0,64},{32,96},{64,0},{96,32},{128,192},{160,224},{192,128},{224,1... | collective-permute-start | bytes 1179656 | tf_op jit(solution)/shard_map/ppermute | solution.py:12
  423.7 40.2 %collective-permute-start.8 = (f32[128,768]{0,1:T(8,128)S(1)}, f32[128,768]{0,1:T(8,128)S(1)}, u32[]{:S(2)}, u32[]{:S(2)}) collective-permute-start(f32[128,768]{0,1:T(8,128)S(1)} %add.137), channel_id=1, source_target_pairs={{0,128},{32,160},{64,192},{96,224},{128,0},{160,32},{192,64},{224,... | collective-permute-start | bytes 1179656 | tf_op jit(solution)/shard_map/ppermute | solution.py:12
  464.7 33.7 %collective-permute-start.9 = (f32[128,768]{0,1:T(8,128)}, f32[128,768]{0,1:T(8,128)}, u32[]{:S(2)}, u32[]{:S(2)}) collective-permute-start(f32[128,768]{0,1:T(8,128)} %add.138), channel_id=1, source_target_pairs={{0,256},{32,288},{64,320},{96,352},{128,384},{160,416},{192,448},{... | collective-permute-start | bytes 1179656 | tf_op jit(solution)/shard_map/ppermute | solution.py:12
  573.4 1.1 copy-start.4
  708.9 13.8 %collective-permute-start.10 = (f32[128,640]{0,1:T(8,128)}, f32[128,640]{0,1:T(8,128)S(1)}, u32[]{:S(2)}, u32[]{:S(2)}) collective-permute-start(f32[128,640]{0,1:T(8,128)} %all-reduce.2.cloned.1.call-done), channel_id=1, source_target_pairs={{0,1},{1,0},{2,3},{3,2},{4,5},{5,4},{6,7},{7,6},{8,9},{9,8},{10,11... | collective-permute-start | bytes 983048 | tf_op jit(solution)/shard_map/ppermute | solution.py:12
Sparse Core Ops, SparseCore 0:
  575.9 133.0 all-reduce.1
where the time goes:
time: 793 us; the launch traced here: 782 us
  waiting for transfers between devices  323 us (41%)
  other arithmetic  310 us (39%)
  starting transfers between devices  77.5 us (10%)
  matrix products  48.2 us (6%)
  between operations  16.1 us (2%)
    ppermute x11, waiting for transfers between devices, from_partner(): return lax.ppermute(value, axis, pairs)  190 us
    another operation x24, other arithmetic, factor_solve(): lax.linalg.triangular_solve(factor, lower_part, left_side=True, lower=Tru...  144 us
    psum x1, waiting for transfers between devices, per_device(): mine = lax.psum(partial_value, 'sub')  133 us
    ppermute x11, starting transfers between devices, from_partner(): return lax.ppermute(value, axis, pairs)  77.5 us
    another operation x18, other arithmetic, core_terms(): schur_factor = jnp.linalg.cholesky(first_inverse - second)  76.9 us
    another operation x18, other arithmetic, core_terms(): first_factor = jnp.linalg.cholesky(first)  76.6 us
  transfers between devices with their start and end apart: 12, of which 12 were waited for; matrix products, arithmetic and copies ran while one was open for 0% of the time, Pallas kernels for 0%

commit v1 on v0

--- a/solution.py
+++ b/solution.py
@@ -4,6 +4,18 @@
 from jax.sharding import PartitionSpec as P
 
 RANK = 128
+
+
+def report_target(arr_in, net_axis):
+    cores_n = lax.axis_size(net_axis)
+    w_next, all_rows = (arr_in, 0)
+    while 1 << all_rows < cores_n:
+        current_block = lax.ppermute(
+            w_next, net_axis, list(map(lambda j0: (j0, j0 ^ 1 << all_rows), range(cores_n)))
+        )
+        w_next = w_next + current_block
+        all_rows = all_rows + 1
+    return w_next
 
 
 def from_partner(value, axis, stride):
@@ -86,7 +98,7 @@
     top = sub_bits + 1
     basis = coupling[:, top * RANK : (top + 1) * RANK]
     partial_value = project_rows(basis, columns)
-    mine = lax.psum(partial_value, "sub")
+    mine = report_target(partial_value, "sub")
     other = from_partner(mine, "leaf", 0)
     is_left = lax.axis_index("leaf") % 2 == 0
     return node_step(columns, mine, other, is_left)

time: 793 us -> 741 us (0.934)
  waiting for transfers between devices: 323 us -> 261 us
  starting transfers between devices: 77.5 us -> 103 us
  between operations: 16.1 us -> 2.81 us
    psum x1 -> x0, waiting for transfers between devices: 133 us -> none  [per_device(): mine = lax.psum(partial_value, 'sub')]
    ppermute x0 -> x4, waiting for transfers between devices: none -> 71.6 us  [report_target(): lax.ppermute(w_next, net_axis, list(map(lambda j0: (j0, j0 ^ 1 << all_row...]
    ppermute x0 -> x4, starting transfers between devices: none -> 35 us  [report_target(): lax.ppermute(w_next, net_axis, list(map(lambda j0: (j0, j0 ^ 1 << all_row...]
    ppermute x11, starting transfers between devices: 77.5 us -> 67.6 us  [from_partner(): return lax.ppermute(value, axis, pairs)]
  transfers between devices with their start and end apart: 12 -> 15, of which waited for: 12 -> 15; matrix products, arithmetic and copies ran while one was open for 0% -> 0% of each run, Pallas kernels for 0% -> 0%
where the time goes in v1:
time: 741 us; the launch traced here: 730 us
  other arithmetic  309 us (42%)
  waiting for transfers between devices  261 us (35%)
  starting transfers between devices  103 us (14%)
  matrix products  47.4 us (6%)
    ppermute x11, waiting for transfers between devices, from_partner(): return lax.ppermute(value, axis, pairs)  190 us
    another operation x24, other arithmetic, factor_solve(): lax.linalg.triangular_solve(factor, lower_part, left_side=True, lower=Tru...  144 us
    another operation x18, other arithmetic, core_terms(): schur_factor = jnp.linalg.cholesky(first_inverse - second)  76.9 us
    another operation x18, other arithmetic, core_terms(): first_factor = jnp.linalg.cholesky(first)  76.6 us
    ppermute x4, waiting for transfers between devices, report_target(): lax.ppermute(w_next, net_axis, list(map(lambda j0: (j0, j0 ^ 1 << all_row...  71.6 us
    ppermute x11, starting transfers between devices, from_partner(): return lax.ppermute(value, axis, pairs)  67.6 us
    ppermute x4, starting transfers between devices, report_target(): lax.ppermute(w_next, net_axis, list(map(lambda j0: (j0, j0 ^ 1 << all_row...  35 us
  transfers between devices with their start and end apart: 15, of which 15 were waited for; matrix products, arithmetic and copies ran while one was open for 0% of the time, Pallas kernels for 0%

profile of v1, /device:TPU:1, one launch (start us, length us, event | category | flops | bytes accessed | tf_op | source)
XLA Modules:
  0.0 729.9 jit_solution(16292803775629360774)
XLA Ops:
  2.7 2.3 divide_convert_fusion
  10.6 11.7 %cholesky.194 = f32[128,128]{1,0:T(8,128)S(1)} custom-call(f32[128,128]{1,0:T(8,128)S(1)} %fusion.114), custom_call_target="Cholesky" | custom-call | tf_op jit(solution)/shard_map/jit(cholesky)/cholesky | solution.py:41
  23.6 9.8 %custom-call.55 = f32[1,128,128]{1,2,0:T(8,128)S(1)} custom-call(f32[1,128,128]{2,1,0:T(8,128)S(1)} %fusion.61), custom_call_target="InvertDiagBlocksLowerTriangular" | custom-call | tf_op jit(solution)/shard_map/triangular_solve/custom-call.2 | solution.py:29
  35.7 11.7 %cholesky.205 = f32[128,128]{1,0:T(8,128)S(1)} custom-call(f32[128,128]{1,0:T(8,128)S(1)} %fusion.111), custom_call_target="Cholesky" | custom-call | tf_op jit(solution)/shard_map/jit(cholesky)/cholesky | solution.py:43
  48.9 9.8 %custom-call.38 = f32[1,128,128]{1,2,0:T(8,128)S(1)} custom-call(f32[1,128,128]{2,1,0:T(8,128)S(1)} %fusion.62), custom_call_target="InvertDiagBlocksLowerTriangular" | custom-call | tf_op jit(solution)/shard_map/triangular_solve | solution.py:29
  64.5 2.0 convolution_bitcast_fusion
  66.5 4.4 collective-permute-start
  70.9 8.5 %collective-permute-done = f32[128,1152]{0,1:T(8,128)S(1)} collective-permute-done((f32[128,1152]{0,1:T(8,128)S(1)}, f32[128,1152]{0,1:T(8,128)S(1)}, u32[]{:S(2)}, u32[]{:S(2)}) %collective-permute-start) | collective-permute-done | bytes 589856 | tf_op jit(solution)/shard_map/ppermute | solution.py:24
  79.6 11.7 %cholesky.216 = f32[128,128]{1,0:T(8,128)S(1)} custom-call(f32[128,128]{1,0:T(8,128)S(1)} %fusion.107), custom_call_target="Cholesky" | custom-call | tf_op jit(solution)/shard_map/jit(cholesky)/cholesky | solution.py:41
  92.7 9.8 %custom-call.57 = f32[1,128,128]{1,2,0:T(8,128)S(1)} custom-call(f32[1,128,128]{2,1,0:T(8,128)S(1)} %fusion.63), custom_call_target="InvertDiagBlocksLowerTriangular" | custom-call | tf_op jit(solution)/shard_map/triangular_solve/custom-call.2 | solution.py:29
  103.8 11.7 %cholesky.227 = f32[128,128]{1,0:T(8,128)S(1)} custom-call(f32[128,128]{1,0:T(8,128)S(1)} %fusion.104), custom_call_target="Cholesky" | custom-call | tf_op jit(solution)/shard_map/jit(cholesky)/cholesky | solution.py:43
  116.8 21.7 %custom-call.39 = f32[1,128,128]{1,2,0:T(8,128)S(1)} custom-call(f32[1,128,128]{2,1,0:T(8,128)S(1)} %fusion.64), custom_call_target="InvertDiagBlocksLowerTriangular" | custom-call | tf_op jit(solution)/shard_map/triangular_solve | solution.py:29
  140.7 2.4 add_convert_fusion
  144.5 4.1 collective-permute-start.1
  148.6 7.0 collective-permute-done.1
  155.7 12.2 %collective-permute-start.2 = (f32[128,1024]{0,1:T(8,128)S(1)}, f32[128,1024]{0,1:T(8,128)}, u32[]{:S(2)}, u32[]{:S(2)}) collective-permute-start(f32[128,1024]{0,1:T(8,128)S(1)} %add.137), channel_id=1, source_target_pairs={{0,64},{32,96},{64,0},{96,32},{128,192},{160,224},{192,128},{224,1... | collective-permute-start | bytes 1572872 | tf_op jit(solution)/shard_map/ppermute | solution.py:24
  167.9 22.9 %collective-permute-done.2 = f32[128,1024]{0,1:T(8,128)} collective-permute-done((f32[128,1024]{0,1:T(8,128)S(1)}, f32[128,1024]{0,1:T(8,128)}, u32[]{:S(2)}, u32[]{:S(2)}) %collective-permute-start.2) | collective-permute-done | bytes 524320 | tf_op jit(solution)/shard_map/ppermute | solution.py:24
  192.0 11.7 %cholesky.238 = f32[128,128]{1,0:T(8,128)S(1)} custom-call(f32[128,128]{1,0:T(8,128)S(1)} %fusion.100), custom_call_target="Cholesky" | custom-call | tf_op jit(solution)/shard_map/jit(cholesky)/cholesky | solution.py:41
  205.1 9.8 %custom-call.59 = f32[1,128,128]{1,2,0:T(8,128)S(1)} custom-call(f32[1,128,128]{2,1,0:T(8,128)S(1)} %fusion.65), custom_call_target="InvertDiagBlocksLowerTriangular" | custom-call | tf_op jit(solution)/shard_map/triangular_solve/custom-call.2 | solution.py:29
  216.1 11.7 %cholesky.249 = f32[128,128]{1,0:T(8,128)S(1)} custom-call(f32[128,128]{1,0:T(8,128)S(1)} %fusion.97), custom_call_target="Cholesky" | custom-call | tf_op jit(solution)/shard_map/jit(cholesky)/cholesky | solution.py:43
  229.2 10.2 %custom-call.40 = f32[1,128,128]{1,2,0:T(8,128)S(1)} custom-call(f32[1,128,128]{2,1,0:T(8,128)S(1)} %fusion.66), custom_call_target="InvertDiagBlocksLowerTriangular" | custom-call | tf_op jit(solution)/shard_map/triangular_solve | solution.py:29
  241.4 2.2 add_convert_fusion.1
  244.4 2.9 collective-permute-start.3
  247.3 9.8 %collective-permute-done.3 = f32[128,896]{0,1:T(8,128)S(1)} collective-permute-done((f32[128,896]{0,1:T(8,128)S(1)}, f32[128,896]{0,1:T(8,128)S(1)}, u32[]{:S(2)}, u32[]{:S(2)}) %collective-permute-start.3) | collective-permute-done | bytes 458784 | tf_op jit(solution)/shard_map/ppermute | solution.py:24
  257.1 5.6 collective-permute-start.4
  262.7 19.9 %collective-permute-done.4 = f32[128,896]{0,1:T(8,128)S(1)} collective-permute-done((f32[128,896]{0,1:T(8,128)S(1)}, f32[128,896]{0,1:T(8,128)S(1)}, u32[]{:S(2)}, u32[]{:S(2)}) %collective-permute-start.4) | collective-permute-done | bytes 458784 | tf_op jit(solution)/shard_map/ppermute | solution.py:24
  282.7 8.8 %collective-permute-start.5 = (f32[128,896]{0,1:T(8,128)S(1)}, f32[128,896]{0,1:T(8,128)S(1)}, u32[]{:S(2)}, u32[]{:S(2)}) collective-permute-start(f32[128,896]{0,1:T(8,128)S(1)} %add.142), channel_id=1, source_target_pairs={{0,128},{32,160},{64,192},{96,224},{128,0},{160,32},{192,64},{224,... | collective-permute-start | bytes 1376264 | tf_op jit(solution)/shard_map/ppermute | solution.py:24
  291.5 39.4 %collective-permute-done.5 = f32[128,896]{0,1:T(8,128)S(1)} collective-permute-done((f32[128,896]{0,1:T(8,128)S(1)}, f32[128,896]{0,1:T(8,128)S(1)}, u32[]{:S(2)}, u32[]{:S(2)}) %collective-permute-start.5) | collective-permute-done | bytes 458784 | tf_op jit(solution)/shard_map/ppermute | solution.py:24
  331.1 11.7 %cholesky.260 = f32[128,128]{1,0:T(8,128)S(1)} custom-call(f32[128,128]{1,0:T(8,128)S(1)} %fusion.93), custom_call_target="Cholesky" | custom-call | tf_op jit(solution)/shard_map/jit(cholesky)/cholesky | solution.py:41
  344.2 9.8 %custom-call.61 = f32[1,128,128]{1,2,0:T(8,128)S(1)} custom-call(f32[1,128,128]{2,1,0:T(8,128)S(1)} %fusion.67), custom_call_target="InvertDiagBlocksLowerTriangular" | custom-call | tf_op jit(solution)/shard_map/triangular_solve/custom-call.2 | solution.py:29
  355.2 11.7 %cholesky.271 = f32[128,128]{1,0:T(8,128)S(1)} custom-call(f32[128,128]{1,0:T(8,128)S(1)} %fusion.90), custom_call_target="Cholesky" | custom-call | tf_op jit(solution)/shard_map/jit(cholesky)/cholesky | solution.py:43
  368.2 9.9 %custom-call.41 = f32[1,128,128]{1,2,0:T(8,128)S(1)} custom-call(f32[1,128,128]{2,1,0:T(8,128)S(1)} %fusion.68), custom_call_target="InvertDiagBlocksLowerTriangular" | custom-call | tf_op jit(solution)/shard_map/triangular_solve | solution.py:29
  380.0 2.1 add_convert_fusion.2
  382.7 1.9 collective-permute-start.6
  384.6 10.1 %collective-permute-done.6 = f32[128,768]{0,1:T(8,128)S(1)} collective-permute-done((f32[128,768]{0,1:T(8,128)S(1)}, f32[128,768]{0,1:T(8,128)S(1)}, u32[]{:S(2)}, u32[]{:S(2)}) %collective-permute-start.6) | collective-permute-done | bytes 393248 | tf_op jit(solution)/shard_map/ppermute | solution.py:24
  394.8 1.9 collective-permute-start.7
  396.7 20.3 %collective-permute-done.7 = f32[128,768]{0,1:T(8,128)S(1)} collective-permute-done((f32[128,768]{0,1:T(8,128)S(1)}, f32[128,768]{0,1:T(8,128)S(1)}, u32[]{:S(2)}, u32[]{:S(2)}) %collective-permute-start.7) | collective-permute-done | bytes 393248 | tf_op jit(solution)/shard_map/ppermute | solution.py:24
  417.1 4.4 collective-permute-start.8
  421.5 35.9 %collective-permute-done.8 = f32[128,768]{0,1:T(8,128)S(1)} collective-permute-done((f32[128,768]{0,1:T(8,128)S(1)}, f32[128,768]{0,1:T(8,128)S(1)}, u32[]{:S(2)}, u32[]{:S(2)}) %collective-permute-start.8) | collective-permute-done | bytes 393248 | tf_op jit(solution)/shard_map/ppermute | solution.py:24
  458.1 19.2 %collective-permute-start.9 = (f32[128,768]{0,1:T(8,128)}, f32[128,768]{0,1:T(8,128)}, u32[]{:S(2)}, u32[]{:S(2)}) collective-permute-start(f32[128,768]{0,1:T(8,128)} %add.148), channel_id=1, source_target_pairs={{0,256},{32,288},{64,320},{96,352},{128,384},{160,416},{192,448},{... | collective-permute-start | bytes 1179656 | tf_op jit(solution)/shard_map/ppermute | solution.py:24
  477.3 14.7 %collective-permute-done.9 = f32[128,768]{0,1:T(8,128)} collective-permute-done((f32[128,768]{0,1:T(8,128)}, f32[128,768]{0,1:T(8,128)}, u32[]{:S(2)}, u32[]{:S(2)}) %collective-permute-start.9) | collective-permute-done | bytes 393248 | tf_op jit(solution)/shard_map/ppermute | solution.py:24
  492.0 1.9 broadcast_select_fusion.7
  497.6 13.2 %cholesky.282 = f32[128,128]{1,0:T(8,128)} custom-call(f32[128,128]{1,0:T(8,128)} %fusion.86), custom_call_target="Cholesky" | custom-call | tf_op jit(solution)/shard_map/jit(cholesky)/cholesky | solution.py:41
  512.3 2.1 fusion.69
  514.4 11.3 %custom-call.63 = f32[1,128,128]{1,2,0:T(8,128)} custom-call(f32[1,128,128]{2,1,0:T(8,128)} %fusion.69), custom_call_target="InvertDiagBlocksLowerTriangular" | custom-call | tf_op jit(solution)/shard_map/triangular_solve/custom-call.2 | solution.py:29
  526.8 2.1 convolution_subtract_fusion.9
  528.9 1.8 convolution_subtract_fusion.13
  533.7 13.2 %cholesky.293 = f32[128,128]{1,0:T(8,128)} custom-call(f32[128,128]{1,0:T(8,128)} %fusion.83), custom_call_target="Cholesky" | custom-call | tf_op jit(solution)/shard_map/jit(cholesky)/cholesky | solution.py:43
  548.5 2.1 fusion.70
  550.6 11.4 %custom-call.42 = f32[1,128,128]{1,2,0:T(8,128)} custom-call(f32[1,128,128]{2,1,0:T(8,128)} %fusion.70), custom_call_target="InvertDiagBlocksLowerTriangular" | custom-call | tf_op jit(solution)/shard_map/triangular_solve | solution.py:29
  567.6 1.9 collective-permute-start.10
  569.5 8.7 %collective-permute-done.10 = f32[128,640]{0,1:T(8,128)S(1)} collective-permute-done((f32[128,640]{0,1:T(8,128)S(1)}, f32[128,640]{0,1:T(8,128)S(1)}, u32[]{:S(2)}, u32[]{:S(2)}) %collective-permute-start.10) | collective-permute-done | bytes 327712 | tf_op jit(solution)/shard_map/ppermute | solution.py:13
  578.3 9.7 %collective-permute-start.11 = (f32[128,640]{0,1:T(8,128)S(1)}, f32[128,640]{0,1:T(8,128)S(1)}, u32[]{:S(2)}, u32[]{:S(2)}) collective-permute-start(f32[128,640]{0,1:T(8,128)S(1)} %add.152), channel_id=1, source_target_pairs={{0,64},{32,96},{64,0},{96,32},{128,192},{160,224},{192,128},{224,1... | collective-permute-start | bytes 983048 | tf_op jit(solution)/shard_map/ppermute | solution.py:13
  588.0 14.3 %collective-permute-done.11 = f32[128,640]{0,1:T(8,128)S(1)} collective-permute-done((f32[128,640]{0,1:T(8,128)S(1)}, f32[128,640]{0,1:T(8,128)S(1)}, u32[]{:S(2)}, u32[]{:S(2)}) %collective-permute-start.11) | collective-permute-done | bytes 327712 | tf_op jit(solution)/shard_map/ppermute | solution.py:13
  602.3 6.9 collective-permute-start.12
  609.2 28.6 %collective-permute-done.12 = f32[128,640]{0,1:T(8,128)S(1)} collective-permute-done((f32[128,640]{0,1:T(8,128)S(1)}, f32[128,640]{0,1:T(8,128)S(1)}, u32[]{:S(2)}, u32[]{:S(2)}) %collective-permute-start.12) | collective-permute-done | bytes 327712 | tf_op jit(solution)/shard_map/ppermute | solution.py:13
  637.9 16.5 %collective-permute-start.13 = (f32[128,640]{0,1:T(8,128)S(1)}, f32[128,640]{0,1:T(8,128)S(1)}, u32[]{:S(2)}, u32[]{:S(2)}) collective-permute-start(f32[128,640]{0,1:T(8,128)S(1)} %add.154), channel_id=1, source_target_pairs={{0,256},{32,288},{64,320},{96,352},{128,384},{160,416},{192,448},{... | collective-permute-start | bytes 983048 | tf_op jit(solution)/shard_map/ppermute | solution.py:13
  654.4 20.1 %collective-permute-done.13 = f32[128,640]{0,1:T(8,128)S(1)} collective-permute-done((f32[128,640]{0,1:T(8,128)S(1)}, f32[128,640]{0,1:T(8,128)S(1)}, u32[]{:S(2)}, u32[]{:S(2)}) %collective-permute-start.13) | collective-permute-done | bytes 327712 | tf_op jit(solution)/shard_map/ppermute | solution.py:13
  674.5 2.4 collective-permute-start.14
  678.3 11.7 %cholesky.304 = f32[128,128]{1,0:T(8,128)S(1)} custom-call(f32[128,128]{1,0:T(8,128)S(1)} %fusion.79), custom_call_target="Cholesky" | custom-call | tf_op jit(solution)/shard_map/jit(cholesky)/cholesky | solution.py:41
  691.4 9.8 %custom-call.65 = f32[1,128,128]{1,2,0:T(8,128)S(1)} custom-call(f32[1,128,128]{2,1,0:T(8,128)S(1)} %fusion.71), custom_call_target="InvertDiagBlocksLowerTriangular" | custom-call | tf_op jit(solution)/shard_map/triangular_solve/custom-call.2 | solution.py:29
  702.3 11.7 %cholesky.315 = f32[128,128]{1,0:T(8,128)S(1)} custom-call(f32[128,128]{1,0:T(8,128)S(1)} %fusion.76), custom_call_target="Cholesky" | custom-call | tf_op jit(solution)/shard_map/jit(cholesky)/cholesky | solution.py:43
  715.3 10.0 %custom-call.43 = f32[1,128,128]{1,2,0:T(8,128)S(1)} custom-call(f32[1,128,128]{2,1,0:T(8,128)S(1)} %fusion.72), custom_call_target="InvertDiagBlocksLowerTriangular" | custom-call | tf_op jit(solution)/shard_map/triangular_solve | solution.py:29
  726.8 2.7 add_convert_fusion.4
  (139 shorter events, 63.6 us)
Async XLA Ops:
  8.2 0.8 copy-start.5
  64.5 2.0 copy-start
  66.5 12.9 %collective-permute-start = (f32[128,1152]{0,1:T(8,128)S(1)}, f32[128,1152]{0,1:T(8,128)S(1)}, u32[]{:S(2)}, u32[]{:S(2)}) collective-permute-start(f32[128,1152]{0,1:T(8,128)S(1)} %convolution_bitcast_fusion), channel_id=1, source_target_pairs={{0,32},{32,0},{64,96},{96,64},{128,160},{160,128},{192,224},{224,1... | collective-permute-start | bytes 1769480 | tf_op jit(solution)/shard_map/ppermute | solution.py:24
  140.1 3.0 copy-start.1
  143.2 1.4 copy-start.2
  144.5 11.1 %collective-permute-start.1 = (f32[128,1024]{0,1:T(8,128)S(1)}, f32[128,1024]{0,1:T(8,128)S(1)}, u32[]{:S(2)}, u32[]{:S(2)}) collective-permute-start(f32[128,1024]{0,1:T(8,128)S(1)} %convolution_bitcast_fusion.1), channel_id=1, source_target_pairs={{0,32},{32,0},{64,96},{96,64},{128,160},{160,128},{192,224},{224,1... | collective-permute-start | bytes 1572872 | tf_op jit(solution)/shard_map/ppermute | solution.py:24
  155.7 35.1 %collective-permute-start.2 = (f32[128,1024]{0,1:T(8,128)S(1)}, f32[128,1024]{0,1:T(8,128)}, u32[]{:S(2)}, u32[]{:S(2)}) collective-permute-start(f32[128,1024]{0,1:T(8,128)S(1)} %add.137), channel_id=1, source_target_pairs={{0,64},{32,96},{64,0},{96,32},{128,192},{160,224},{192,128},{224,1... | collective-permute-start | bytes 1572872 | tf_op jit(solution)/shard_map/ppermute | solution.py:24
  243.7 39.0 %copy-start.3 = (bf16[1024,896]{1,0:T(8,128)(2,1)}, bf16[1024,896]{1,0:T(8,128)(2,1)S(1)}, u32[]{:S(2)}) copy-start(bf16[1024,896]{1,0:T(8,128)(2,1)S(1)} %add_convert_fusion.1) | copy-start | bytes 5505028
  244.4 12.7 %collective-permute-start.3 = (f32[128,896]{0,1:T(8,128)S(1)}, f32[128,896]{0,1:T(8,128)S(1)}, u32[]{:S(2)}, u32[]{:S(2)}) collective-permute-start(f32[128,896]{0,1:T(8,128)S(1)} %convolution_bitcast_fusion.2), channel_id=1, source_target_pairs={{0,32},{32,0},{64,96},{96,64},{128,160},{160,128},{192,224},{224,1... | collective-permute-start | bytes 1376264 | tf_op jit(solution)/shard_map/ppermute | solution.py:24
  257.1 25.5 %collective-permute-start.4 = (f32[128,896]{0,1:T(8,128)S(1)}, f32[128,896]{0,1:T(8,128)S(1)}, u32[]{:S(2)}, u32[]{:S(2)}) collective-permute-start(f32[128,896]{0,1:T(8,128)S(1)} %add.141), channel_id=1, source_target_pairs={{0,64},{32,96},{64,0},{96,32},{128,192},{160,224},{192,128},{224,1... | collective-permute-start | bytes 1376264 | tf_op jit(solution)/shard_map/ppermute | solution.py:24
  282.7 48.2 %collective-permute-start.5 = (f32[128,896]{0,1:T(8,128)S(1)}, f32[128,896]{0,1:T(8,128)S(1)}, u32[]{:S(2)}, u32[]{:S(2)}) collective-permute-start(f32[128,896]{0,1:T(8,128)S(1)} %add.142), channel_id=1, source_target_pairs={{0,128},{32,160},{64,192},{96,224},{128,0},{160,32},{192,64},{224,... | collective-permute-start | bytes 1376264 | tf_op jit(solution)/shard_map/ppermute | solution.py:24
  382.7 12.1 %collective-permute-start.6 = (f32[128,768]{0,1:T(8,128)S(1)}, f32[128,768]{0,1:T(8,128)S(1)}, u32[]{:S(2)}, u32[]{:S(2)}) collective-permute-start(f32[128,768]{0,1:T(8,128)S(1)} %convolution_bitcast_fusion.3), channel_id=1, source_target_pairs={{0,32},{32,0},{64,96},{96,64},{128,160},{160,128},{192,224},{224,1... | collective-permute-start | bytes 1179656 | tf_op jit(solution)/shard_map/ppermute | solution.py:24
  394.8 22.2 %collective-permute-start.7 = (f32[128,768]{0,1:T(8,128)S(1)}, f32[128,768]{0,1:T(8,128)S(1)}, u32[]{:S(2)}, u32[]{:S(2)}) collective-permute-start(f32[128,768]{0,1:T(8,128)S(1)} %add.146), channel_id=1, source_target_pairs={{0,64},{32,96},{64,0},{96,32},{128,192},{160,224},{192,128},{224,1... | collective-permute-start | bytes 1179656 | tf_op jit(solution)/shard_map/ppermute | solution.py:24
  417.1 40.2 %collective-permute-start.8 = (f32[128,768]{0,1:T(8,128)S(1)}, f32[128,768]{0,1:T(8,128)S(1)}, u32[]{:S(2)}, u32[]{:S(2)}) collective-permute-start(f32[128,768]{0,1:T(8,128)S(1)} %add.147), channel_id=1, source_target_pairs={{0,128},{32,160},{64,192},{96,224},{128,0},{160,32},{192,64},{224,... | collective-permute-start | bytes 1179656 | tf_op jit(solution)/shard_map/ppermute | solution.py:24
  458.1 33.9 %collective-permute-start.9 = (f32[128,768]{0,1:T(8,128)}, f32[128,768]{0,1:T(8,128)}, u32[]{:S(2)}, u32[]{:S(2)}) collective-permute-start(f32[128,768]{0,1:T(8,128)} %add.148), channel_id=1, source_target_pairs={{0,256},{32,288},{64,320},{96,352},{128,384},{160,416},{192,448},{... | collective-permute-start | bytes 1179656 | tf_op jit(solution)/shard_map/ppermute | solution.py:24
  567.1 70.8 %copy-start.4 = (bf16[1024,640]{1,0:T(8,128)(2,1)}, bf16[1024,640]{1,0:T(8,128)(2,1)S(1)}, u32[]{:S(2)}) copy-start(bf16[1024,640]{1,0:T(8,128)(2,1)S(1)} %add_convert_fusion.3) | copy-start | bytes 3932164
  567.6 10.6 %collective-permute-start.10 = (f32[128,640]{0,1:T(8,128)S(1)}, f32[128,640]{0,1:T(8,128)S(1)}, u32[]{:S(2)}, u32[]{:S(2)}) collective-permute-start(f32[128,640]{0,1:T(8,128)S(1)} %convolution_bitcast_fusion.4), channel_id=1, source_target_pairs={{0,32},{32,0},{64,96},{96,64},{128,160},{160,128},{192,224},{224,1... | collective-permute-start | bytes 983048 | tf_op jit(solution)/shard_map/ppermute | solution.py:13
  578.3 24.0 %collective-permute-start.11 = (f32[128,640]{0,1:T(8,128)S(1)}, f32[128,640]{0,1:T(8,128)S(1)}, u32[]{:S(2)}, u32[]{:S(2)}) collective-permute-start(f32[128,640]{0,1:T(8,128)S(1)} %add.152), channel_id=1, source_target_pairs={{0,64},{32,96},{64,0},{96,32},{128,192},{160,224},{192,128},{224,1... | collective-permute-start | bytes 983048 | tf_op jit(solution)/shard_map/ppermute | solution.py:13
  602.3 35.5 %collective-permute-start.12 = (f32[128,640]{0,1:T(8,128)S(1)}, f32[128,640]{0,1:T(8,128)S(1)}, u32[]{:S(2)}, u32[]{:S(2)}) collective-permute-start(f32[128,640]{0,1:T(8,128)S(1)} %add.153), channel_id=1, source_target_pairs={{0,128},{32,160},{64,192},{96,224},{128,0},{160,32},{192,64},{224,... | collective-permute-start | bytes 983048 | tf_op jit(solution)/shard_map/ppermute | solution.py:13
  637.9 36.6 %collective-permute-start.13 = (f32[128,640]{0,1:T(8,128)S(1)}, f32[128,640]{0,1:T(8,128)S(1)}, u32[]{:S(2)}, u32[]{:S(2)}) collective-permute-start(f32[128,640]{0,1:T(8,128)S(1)} %add.154), channel_id=1, source_target_pairs={{0,256},{32,288},{64,320},{96,352},{128,384},{160,416},{192,448},{... | collective-permute-start | bytes 983048 | tf_op jit(solution)/shard_map/ppermute | solution.py:13
  674.5 3.7 collective-permute-start.14
